TPU v7x, 32 devices: a whole 2x2x4 slice. The times are simulated.
32 devices in a mesh: blk: 16 (over z, x, core), sub: 2 (over y).
Axes of the slice: x: 2, y: 2, z: 4, core: 2. Of those that a mesh axis runs over, the one named last changes fastest.
Arguments:
- vectors: bfloat16 [16, 131072], P('sub', 'blk')
- energies: float32 [131072], P('blk'), may hold values from 1 to 4
- tile_values: bfloat16 [16, 128, 128, 128], P('blk', 'sub'), may hold values from -0.1875 to 0.1875
- tile_rows: int32 [16, 128], P('blk', 'sub'), may hold values from 0 to 63
- tile_cols: int32 [16, 128], P('blk', 'sub'), may hold values from 0 to 63
- tile_offsets: int32 [16, 128], P('blk', 'sub'), may hold values from 0 to 2, as said below
- tile_count: int32 [16, 2], P('blk', 'sub'), may hold values from 8 to 64, as said below
Outputs:
- residual: float32 [16, 131072], P('sub', 'blk')
Inputs may be any that keep to these rules, and one draw needn't show every extreme that they name: `tile_offsets`: an offset never exceeds the row block's index b; where the offset is 0, tile_rows >= tile_cols. `tile_count`: each count is 64 divided by 1, 2, 4 or 8.
All inputs are finite; a program needn't handle non-finite values.
Results may differ from a plain program's by a relative error of at most 0.0003.
Values may be sent and summed in bfloat16 or wider, within the bound.
No kernel may reach another device: no remote copies, remote signals or barrier semaphores. Data moves between devices by JAX's collectives and lax.ppermute only.
A program may use at most 64 MiB of HBM per device.

v0:
```python
import jax
import jax.numpy as jnp
from jax import lax
from jax.sharding import PartitionSpec as P

BW = 2


def from_behind(value, axis, steps):
    count = lax.axis_size(axis)
    first, last = (max(0, -steps), min(count, count - steps))
    return lax.ppermute(value, axis, [(source, source + steps) for source in range(first, last)])


def ritz_coefficients(gram, projected):
    lower = jnp.linalg.cholesky(gram)
    half = lax.linalg.triangular_solve(lower, projected, left_side=True, lower=True)
    return lax.linalg.triangular_solve(lower, half, left_side=True, lower=True, transpose_a=True)


def tile_products(tile_vals, row_ids, col_ids, offset_ids, live, stacked, own_block):
    width, rows_dev = own_block.shape
    tile_side = tile_vals.shape[-1]
    row_tiles = rows_dev // tile_side
    depth = stacked.shape[0]
    highest = lax.Precision.HIGHEST
    grid_view = stacked.reshape(depth, width, row_tiles, tile_side)
    sources = grid_view[offset_ids, :, col_ids, :]
    direct_terms = jnp.einsum(
        "tij,tcj->tci", tile_vals, sources, preferred_element_type=jnp.float32
    )
    own_tiles = own_block.reshape(width, row_tiles, tile_side)[:, row_ids, :]
    mirror_terms = jnp.einsum(
        "tji,ctj->tci", tile_vals, own_tiles, preferred_element_type=jnp.float32
    )
    tile_range = jnp.arange(row_tiles, dtype=jnp.int32)
    row_hot = (row_ids[:, None] == tile_range[None, :]).astype(jnp.float32) * live[:, None]
    col_hot = (col_ids[:, None] == tile_range[None, :]).astype(jnp.float32) * live[:, None]
    depth_hot = (offset_ids[:, None] == jnp.arange(depth, dtype=jnp.int32)[None, :]).astype(
        jnp.float32
    )
    direct = jnp.einsum("tci,tr->cri", direct_terms, row_hot, precision=highest).reshape(
        width, rows_dev
    )
    mirror = jnp.einsum("tci,tk,tr->kcri", mirror_terms, depth_hot, col_hot, precision=highest)
    return (direct, mirror.reshape(depth, width, rows_dev))


def send_back(pieces):
    gathered_sum = pieces[0]
    for offset in range(1, BW + 1):
        gathered_sum = gathered_sum + from_behind(pieces[offset], "blk", -offset)
    return gathered_sum


def on_device(vectors, energies, tile_values, tile_rows, tile_cols, tile_offsets, tile_count):
    columns = vectors.shape[0]
    part_index = lax.axis_index("sub")
    tile_vals = tile_values[0]
    row_ids = tile_rows[0]
    col_ids = tile_cols[0]
    offset_ids = tile_offsets[0]
    live_count = tile_count[0, 0]
    slots = tile_vals.shape[0]
    whole = lax.all_gather(vectors, "sub", axis=0, tiled=True)
    lowered = [whole]
    for offset in range(1, BW + 1):
        lowered.append(from_behind(whole, "blk", offset))
    stacked = jnp.stack(lowered, 0)
    own_block = stacked[0]
    width, rows_dev = own_block.shape
    live = (jnp.arange(slots, dtype=jnp.int32) < live_count).astype(jnp.float32)
    direct, mirror = tile_products(
        tile_vals, row_ids, col_ids, offset_ids, live, stacked, own_block
    )
    mirror = mirror.at[0].add(direct)
    applied = lax.psum_scatter(send_back(mirror), "sub", scatter_dimension=0, tiled=True)
    applied = applied + energies[None, :] * vectors.astype(jnp.float32)
    highest = lax.Precision.HIGHEST
    own_wide = own_block.astype(jnp.float32)
    gram_part = jnp.dot(own_block, vectors.T, preferred_element_type=jnp.float32)
    proj_part = jnp.dot(own_wide, applied.T, precision=highest)
    empty = jnp.zeros((width, width), jnp.float32)
    gram_full = lax.dynamic_update_slice(empty, gram_part, (0, part_index * columns))
    proj_full = lax.dynamic_update_slice(empty, proj_part, (0, part_index * columns))
    gram, projected = lax.psum((gram_full, proj_full), ("blk", "sub"))
    coefficients = ritz_coefficients(gram, projected)
    mine = lax.dynamic_slice_in_dim(coefficients, part_index * columns, columns, 1)
    return applied - jnp.dot(mine.T, own_wide, precision=highest)


def solution(mesh):
    in_specs = (
        P("sub", "blk"),
        P("blk"),
        P("blk", "sub", None, None),
        P("blk", "sub"),
        P("blk", "sub"),
        P("blk", "sub"),
        P("blk", "sub"),
    )
    out_specs = P("sub", "blk")
    return jax.shard_map(
        on_device, mesh=mesh, in_specs=in_specs, out_specs=out_specs, check_vma=False
    )
```

profile of v0, /device:TPU:0, one launch (start us, length us, event | category | flops | bytes accessed | tf_op | source)
XLA Modules:
  0.0 120.7 jit_solution(16180372393465413950)
XLA Ops:
  6.5 7.5 %all_gather.3 = bf16[16,8192]{1,0:T(8,128)(2,1)S(1)} all-gather(bf16[8,8192]{1,0:T(8,128)(2,1)} %param.9), channel_id=1, replica_groups=mesh['blk'=16,'sub'=2] {'sub'}, dimensions={0}, use_global_device_ids=true | all-gather | bytes 393216 | tf_op jit(solution)/shard_map/all_gather | solution.py:65
  14.1 3.6 %collective-permute-start.1 = (bf16[16,8192]{1,0:T(8,128)(2,1)S(1)}, bf16[16,8192]{1,0:T(8,128)(2,1)S(1)}, u32[]{:S(2)}, u32[]{:S(2)}) collective-permute-start(bf16[16,8192]{1,0:T(8,128)(2,1)S(1)} %all_gather.3), channel_id=1, source_target_pairs={{0,4},{2,6},{4,8},{6,10},{8,12},{10,14},{12,16},{14,18},{16,20},{1... | collective-permute-start | bytes 786440 | tf_op jit(solution)/shard_map/ppermute | solution.py:12
  17.6 1.3 %collective-permute-start = (bf16[16,8192]{1,0:T(8,128)(2,1)S(1)}, bf16[16,8192]{1,0:T(8,128)(2,1)S(1)}, u32[]{:S(2)}, u32[]{:S(2)}) collective-permute-start(bf16[16,8192]{1,0:T(8,128)(2,1)S(1)} %all_gather.3), channel_id=1, source_target_pairs={{0,2},{2,4},{4,6},{6,8},{8,10},{10,12},{12,14},{14,16},{16,18},{18... | collective-permute-start | bytes 786440 | tf_op jit(solution)/shard_map/ppermute | solution.py:12
  19.0 0.7 fusion.30
  19.7 0.7 fusion.29
  21.0 0.6 gather_fusion
  21.6 0.7 fusion.2
  22.3 1.4 %convolution_bitcast_fusion = f32[3,16,64,128]{3,2,1,0:T(8,128)S(1)} fusion(f32[64,16,128]{2,1,0:T(8,128)S(1)} %fusion.2, f32[64,3]{0,1:T(4,128)S(1)} %fusion.29, f32[64,64]{0,1:T(8,128)S(1)} %fusion.18), kind=kOutput, calls=%fused_computation.7 | convolution fusion | flops 302002176 | bytes 2114304 | tf_op jit(solution)/shard_map/tci,tk,tr->kcri/dot_general | solution.py:45
  23.9 1.1 copy.43
  25.1 1.3 %collective-permute-start.3 = (f32[16,8192]{1,0:T(8,128)}, f32[16,8192]{1,0:T(8,128)}, u32[]{:S(2)}, u32[]{:S(2)}) collective-permute-start(f32[16,8192]{1,0:T(8,128)} %bitcast.93), channel_id=1, source_target_pairs={{4,0},{6,2},{8,4},{10,6},{12,8},{14,10},{16,12},{18,14},{20,16},{2... | collective-permute-start | bytes 1572872 | tf_op jit(solution)/shard_map/ppermute | solution.py:12
  26.3 1.1 copy.44
  27.5 1.3 %collective-permute-start.2 = (f32[16,8192]{1,0:T(8,128)}, f32[16,8192]{1,0:T(8,128)}, u32[]{:S(2)}, u32[]{:S(2)}) collective-permute-start(f32[16,8192]{1,0:T(8,128)} %bitcast.94), channel_id=1, source_target_pairs={{2,0},{4,2},{6,4},{8,6},{10,8},{12,10},{14,12},{16,14},{18,16},{20... | collective-permute-start | bytes 1572872 | tf_op jit(solution)/shard_map/ppermute | solution.py:12
  28.8 0.2 copy.14
  29.1 0.2 copy.16
  29.5 1.0 pad_maximum_fusion
  30.5 1.9 %gather_fusion.1 = bf16[64,16,128]{2,1,0:T(8,128)(2,1)S(1)} fusion(bf16[3,16,64,128]{3,1,2,0:T(8,128)(2,1)} %pad_maximum_fusion, s32[64]{0:T(128)S(1)} %fusion.36), kind=kCustom, calls=%fused_computation.1 | custom fusion | bytes 524800 | tf_op jit(solution)/shard_map/gather | solution.py:28
  32.4 1.2 fusion
  33.6 0.7 fusion.7
  34.3 6.7 %collective-permute-done.3 = f32[16,8192]{1,0:T(8,128)} collective-permute-done((f32[16,8192]{1,0:T(8,128)}, f32[16,8192]{1,0:T(8,128)}, u32[]{:S(2)}, u32[]{:S(2)}) %collective-permute-start.3) | collective-permute-done | bytes 524320 | tf_op jit(solution)/shard_map/ppermute | solution.py:12
  41.0 2.6 %fusion.5 = f32[16,8192]{1,0:T(8,128)} fusion(f32[16,8192]{1,0:T(8,128)} %collective-permute-done.3, f32[16,8192]{1,0:T(8,128)} %collective-permute-done.2, f32[2,8,64,128]{3,2,1,0:T(8,128)S(1)} %bitcast.97, f32[2,8,64,128]{3,2,1,0:T(8,128)S(1)} %bitcast.98), kind=kLoop, calls=%fused_computation.14 | loop fusion | flops 393216 | bytes 2621440 | tf_op jit(solution)/shard_map/add | solution.py:52
  43.7 0.2 fusion.40
  44.1 22.2 %reduce-scatter.2.cloned.1.call-done = f32[8,8192]{1,0:T(8,128)} async-done(((f32[16,8192]{1,0:T(8,128)}), f32[8,8192]{1,0:T(8,128)}) %reduce-scatter.2.cloned.1.call-update) | async-done | bytes 262160 | tf_op jit(solution)/shard_map/reduce_scatter | solution.py:77
  66.3 1.4 %convolution_bitcast_fusion.1 = f32[16,8]{1,0:T(8,128)S(1)} fusion(bf16[16,8192]{1,0:T(8,128)(2,1)S(1)} %all_gather.3, f32[8,8192]{1,0:T(8,128)} %reduce-scatter.2.cloned.1.call-done, bf16[8,8192]{1,0:T(8,128)(2,1)S(1)} %copy-done.1, f32[8192]{0:T(1024)S(1)} %copy-done.2), kind=kOutput, calls=%fused_computation.8 | convolution fusion | flops 12779520 | bytes 688640 | tf_op jit(solution)/shard_map/dot_general | solution.py:82
  67.7 0.2 dynamic_update_slice.7
  67.9 39.5 %all-reduce = (f32[16,16]{1,0:T(8,128)S(1)}, f32[16,16]{1,0:T(8,128)S(1)}) all-reduce(f32[16,16]{1,0:T(8,128)S(1)} %dynamic_update_slice.7, f32[16,16]{1,0:T(8,128)S(1)} %dynamic_update_slice.6), channel_id=1, replica_groups=mesh['blk'=16,'sub'=2] {'blk','sub'}, use_global_device_ids=true, to_apply=%region_4.5 | all-reduce | flops 512 | bytes 4096 | tf_op jit(solution)/shard_map/psum | solution.py:86
  107.5 1.5 %cholesky.15 = f32[16,16]{1,0:T(8,128)S(1)} custom-call(f32[16,16]{1,0:T(8,128)S(1)} %fusion.27), custom_call_target="Cholesky" | custom-call | tf_op jit(solution)/shard_map/jit(cholesky)/cholesky | solution.py:16
  109.0 0.6 compare_reduce_fusion
  109.6 0.6 fusion.22
  110.3 1.2 %custom-call.8 = f32[1,16,16]{1,2,0:T(8,128)S(1)} custom-call(f32[1,16,16]{2,1,0:T(8,128)S(1)} %fusion.22), custom_call_target="InvertDiagBlocksLowerTriangular" | custom-call | tf_op jit(solution)/shard_map/triangular_solve | solution.py:18
  111.5 0.2 fusion.25
  111.7 0.2 fusion.23
  111.9 1.9 %convolution_subtract_fusion = f32[8,8192]{1,0:T(8,128)} fusion(bf16[16,8192]{1,0:T(8,128)(2,1)S(1)} %all_gather.3, f32[8,8192]{1,0:T(8,128)} %reduce-scatter.2.cloned.1.call-done, bf16[8,8192]{1,0:T(8,128)(2,1)S(1)} %copy-done.1, f32[8192]{0:T(1024)S(1)} %copy-done.2, f32[16,16]{0,1:T(8,128)S(1)} %fusion.23, s32[]{:T(128)S(6)} %select_n.42), kind=kOutput, calls=%fused_computation.2 | convolution fusion | flops 12845056 | bytes 954372 | tf_op jit(solution)/shard_map/dot_general | solution.py:89
  (33 shorter events, 0.9 us)
Async XLA Ops:
  6.5 15.1 %copy-start = (bf16[1,64,128,128]{3,2,1,0:T(8,128)(2,1)S(1)}, bf16[1,64,128,128]{3,2,1,0:T(8,128)(2,1)}, u32[]{:S(2)}) copy-start(bf16[1,64,128,128]{3,2,1,0:T(8,128)(2,1)} %param.11) | copy-start | bytes 6291460
  6.5 15.8 %copy-start.4 = (s32[1,64]{1,0:T(1,128)S(1)}, s32[1,64]{1,0:T(1,128)}, u32[]{:S(2)}) copy-start(s32[1,64]{1,0:T(1,128)} %param.13) | copy-start | bytes 772
  6.5 59.7 %reduce-scatter.2.cloned.1.call-start = ((), (), s32[]{:S(2)}) async-start(), calls=%async_computation.1 | async-start | bytes 786432 | tf_op jit(solution)/shard_map/reduce_scatter | solution.py:77
  14.1 14.9 %collective-permute-start.1 = (bf16[16,8192]{1,0:T(8,128)(2,1)S(1)}, bf16[16,8192]{1,0:T(8,128)(2,1)S(1)}, u32[]{:S(2)}, u32[]{:S(2)}) collective-permute-start(bf16[16,8192]{1,0:T(8,128)(2,1)S(1)} %all_gather.3), channel_id=1, source_target_pairs={{0,4},{2,6},{4,8},{6,10},{8,12},{10,14},{12,16},{14,18},{16,20},{1... | collective-permute-start | bytes 786440 | tf_op jit(solution)/shard_map/ppermute | solution.py:12
  17.6 11.6 %collective-permute-start = (bf16[16,8192]{1,0:T(8,128)(2,1)S(1)}, bf16[16,8192]{1,0:T(8,128)(2,1)S(1)}, u32[]{:S(2)}, u32[]{:S(2)}) collective-permute-start(bf16[16,8192]{1,0:T(8,128)(2,1)S(1)} %all_gather.3), channel_id=1, source_target_pairs={{0,2},{2,4},{4,6},{6,8},{8,10},{10,12},{12,14},{14,16},{16,18},{18... | collective-permute-start | bytes 786440 | tf_op jit(solution)/shard_map/ppermute | solution.py:12
  23.9 5.1 %copy-start.5 = (s32[1,64]{1,0:T(1,128)S(1)}, s32[1,64]{1,0:T(1,128)}, u32[]{:S(2)}) copy-start(s32[1,64]{1,0:T(1,128)} %param.14) | copy-start | bytes 772
  25.1 16.0 %collective-permute-start.3 = (f32[16,8192]{1,0:T(8,128)}, f32[16,8192]{1,0:T(8,128)}, u32[]{:S(2)}, u32[]{:S(2)}) collective-permute-start(f32[16,8192]{1,0:T(8,128)} %bitcast.93), channel_id=1, source_target_pairs={{4,0},{6,2},{8,4},{10,6},{12,8},{14,10},{16,12},{18,14},{20,16},{2... | collective-permute-start | bytes 1572872 | tf_op jit(solution)/shard_map/ppermute | solution.py:12
  27.5 13.6 %collective-permute-start.2 = (f32[16,8192]{1,0:T(8,128)}, f32[16,8192]{1,0:T(8,128)}, u32[]{:S(2)}, u32[]{:S(2)}) collective-permute-start(f32[16,8192]{1,0:T(8,128)} %bitcast.94), channel_id=1, source_target_pairs={{2,0},{4,2},{6,4},{8,6},{10,8},{12,10},{14,12},{16,14},{18,16},{20... | collective-permute-start | bytes 1572872 | tf_op jit(solution)/shard_map/ppermute | solution.py:12
  30.5 3.1 %copy-start.3 = (s32[1,64]{1,0:T(1,128)S(1)}, s32[1,64]{1,0:T(1,128)}, u32[]{:S(2)}) copy-start(s32[1,64]{1,0:T(1,128)} %param.12) | copy-start | bytes 772
  33.6 10.1 %copy-start.1 = (bf16[8,8192]{1,0:T(8,128)(2,1)S(1)}, bf16[8,8192]{1,0:T(8,128)(2,1)}, u32[]{:S(2)}) copy-start(bf16[8,8192]{1,0:T(8,128)(2,1)} %param.9) | copy-start | bytes 393220
  33.6 32.7 %copy-start.2 = (f32[8192]{0:T(1024)S(1)}, f32[8192]{0:T(1024)}, u32[]{:S(2)}) copy-start(f32[8192]{0:T(1024)} %param.10) | copy-start | bytes 98308
Sparse Core Ops, SparseCore 0:
  43.8 22.4 reduce-scatter.1
where the time goes:
time: 121 us
  blocking collectives  47 us (39%)
  waiting for transfers between devices  28.9 us (24%)
  between operations  14.3 us (12%)
  other arithmetic  8.95 us (7%)
  matrix products  7.91 us (7%)
  starting transfers between devices  7.45 us (6%)
  local copies, waits for them, and re-layouts  6.14 us (5%)
    psum x1, blocking collectives, on_device(): gram, projected = lax.psum((gram_full, proj_full), ('blk', 'sub'))  39.5 us
    reduce_scatter x1, waiting for transfers between devices, on_device(): lax.psum_scatter(send_back(mirror), 'sub', scatter_dimension=0, tiled=True)  22.2 us
    all_gather x1, blocking collectives, on_device(): whole = lax.all_gather(vectors, 'sub', axis=0, tiled=True)  7.51 us
    ppermute x4, starting transfers between devices, from_behind(): lax.ppermute(value, axis, [(source, source + steps) for source in range(f...  7.45 us
    ppermute x4, waiting for transfers between devices, from_behind(): lax.ppermute(value, axis, [(source, source + steps) for source in range(f...  6.71 us
    add x1, other arithmetic, send_back(): gathered_sum = gathered_sum + from_behind(pieces[offset], 'blk', -offset)  2.61 us
  transfers between devices with their start and end apart: 5, of which 2 were waited for; matrix products, arithmetic and copies ran while one was open for 10% of the time, Pallas kernels for 0%

commit v1 on v0

--- a/solution.py
+++ b/solution.py
@@ -83,7 +83,8 @@
     empty = jnp.zeros((width, width), jnp.float32)
     gram_full = lax.dynamic_update_slice(empty, gram_part, (0, part_index * columns))
     proj_full = lax.dynamic_update_slice(empty, proj_part, (0, part_index * columns))
-    gram, projected = lax.psum((gram_full, proj_full), ("blk", "sub"))
+    slot_build = lambda raw: lax.psum(lax.psum(raw, "sub"), "blk")
+    gram, projected = slot_build((gram_full, proj_full))
     coefficients = ritz_coefficients(gram, projected)
     mine = lax.dynamic_slice_in_dim(coefficients, part_index * columns, columns, 1)
     return applied - jnp.dot(mine.T, own_wide, precision=highest)

time: 121 us -> 148 us (1.22)
  blocking collectives: 47 us -> 73.9 us
    psum x1 -> x2, blocking collectives: 39.5 us -> 66.4 us  [on_device(): slot_build = lambda raw: lax.psum(lax.psum(raw, 'sub'), 'blk')]
  transfers between devices with their start and end apart: 5 -> 5, of which waited for: 2 -> 2; matrix products, arithmetic and copies ran while one was open for 10% -> 8% of each run, Pallas kernels for 0% -> 0%
where the time goes in v1:
time: 148 us
  blocking collectives  73.9 us (50%)
  waiting for transfers between devices  28.9 us (20%)
  between operations  14.3 us (10%)
  other arithmetic  8.93 us (6%)
  matrix products  7.9 us (5%)
  starting transfers between devices  7.45 us (5%)
  local copies, waits for them, and re-layouts  6.15 us (4%)
    psum x2, blocking collectives, on_device(): slot_build = lambda raw: lax.psum(lax.psum(raw, 'sub'), 'blk')  66.4 us
    reduce_scatter x1, waiting for transfers between devices, on_device(): lax.psum_scatter(send_back(mirror), 'sub', scatter_dimension=0, tiled=True)  22.2 us
    all_gather x1, blocking collectives, on_device(): whole = lax.all_gather(vectors, 'sub', axis=0, tiled=True)  7.51 us
    ppermute x4, starting transfers between devices, from_behind(): lax.ppermute(value, axis, [(source, source + steps) for source in range(f...  7.45 us
    ppermute x4, waiting for transfers between devices, from_behind(): lax.ppermute(value, axis, [(source, source + steps) for source in range(f...  6.71 us
  transfers between devices with their start and end apart: 5, of which 2 were waited for; matrix products, arithmetic and copies ran while one was open for 8% of the time, Pallas kernels for 0%

profile of v1, /device:TPU:0, one launch (start us, length us, event | category | flops | bytes accessed | tf_op | source)
XLA Modules:
  0.0 147.6 jit_solution(7460387213883948146)
XLA Ops:
  6.5 7.5 %all_gather.3 = bf16[16,8192]{1,0:T(8,128)(2,1)S(1)} all-gather(bf16[8,8192]{1,0:T(8,128)(2,1)} %param.9), channel_id=1, replica_groups=mesh['blk'=16,'sub'=2] {'sub'}, dimensions={0}, use_global_device_ids=true | all-gather | bytes 393216 | tf_op jit(solution)/shard_map/all_gather | solution.py:65
  14.1 3.6 %collective-permute-start.1 = (bf16[16,8192]{1,0:T(8,128)(2,1)S(1)}, bf16[16,8192]{1,0:T(8,128)(2,1)S(1)}, u32[]{:S(2)}, u32[]{:S(2)}) collective-permute-start(bf16[16,8192]{1,0:T(8,128)(2,1)S(1)} %all_gather.3), channel_id=1, source_target_pairs={{0,4},{2,6},{4,8},{6,10},{8,12},{10,14},{12,16},{14,18},{16,20},{1... | collective-permute-start | bytes 786440 | tf_op jit(solution)/shard_map/ppermute | solution.py:12
  17.6 1.3 collective-permute-start
  19.0 0.7 fusion.30
  19.7 0.7 fusion.29
  21.0 0.6 gather_fusion
  21.6 0.7 fusion.2
  22.3 1.4 convolution_bitcast_fusion
  23.9 1.1 copy.43
  25.0 1.3 collective-permute-start.3
  26.3 1.1 copy.44
  27.5 1.3 collective-permute-start.2
  28.8 0.2 copy.14
  29.5 1.0 pad_maximum_fusion
  30.5 1.9 %gather_fusion.1 = bf16[64,16,128]{2,1,0:T(8,128)(2,1)S(1)} fusion(bf16[3,16,64,128]{3,1,2,0:T(8,128)(2,1)} %pad_maximum_fusion, s32[64]{0:T(128)S(1)} %fusion.36), kind=kCustom, calls=%fused_computation.1 | custom fusion | bytes 524800 | tf_op jit(solution)/shard_map/gather | solution.py:28
  32.4 1.2 fusion
  33.6 0.7 fusion.7
  34.3 6.7 %collective-permute-done.3 = f32[16,8192]{1,0:T(8,128)} collective-permute-done((f32[16,8192]{1,0:T(8,128)}, f32[16,8192]{1,0:T(8,128)}, u32[]{:S(2)}, u32[]{:S(2)}) %collective-permute-start.3) | collective-permute-done | bytes 524320 | tf_op jit(solution)/shard_map/ppermute | solution.py:12
  41.0 2.6 %fusion.5 = f32[16,8192]{1,0:T(8,128)} fusion(f32[16,8192]{1,0:T(8,128)} %collective-permute-done.3, f32[16,8192]{1,0:T(8,128)} %collective-permute-done.2, f32[2,8,64,128]{3,2,1,0:T(8,128)S(1)} %bitcast.97, f32[2,8,64,128]{3,2,1,0:T(8,128)S(1)} %bitcast.98), kind=kLoop, calls=%fused_computation.14 | loop fusion | flops 393216 | bytes 2621440 | tf_op jit(solution)/shard_map/add | solution.py:52
  43.7 0.2 fusion.40
  44.0 22.2 %reduce-scatter.2.cloned.1.call-done = f32[8,8192]{1,0:T(8,128)} async-done(((f32[16,8192]{1,0:T(8,128)}), f32[8,8192]{1,0:T(8,128)}) %reduce-scatter.2.cloned.1.call-update) | async-done | bytes 262160 | tf_op jit(solution)/shard_map/reduce_scatter | solution.py:77
  66.3 1.4 convolution_bitcast_fusion.1
  67.7 0.2 dynamic_update_slice.7
  67.9 7.0 %all-reduce.1 = (f32[16,16]{1,0:T(8,128)S(1)}, f32[16,16]{1,0:T(8,128)S(1)}) all-reduce(f32[16,16]{1,0:T(8,128)S(1)} %dynamic_update_slice.7, f32[16,16]{1,0:T(8,128)S(1)} %dynamic_update_slice.6), channel_id=1, replica_groups=mesh['blk'=16,'sub'=2] {'sub'}, use_global_device_ids=true, to_apply=%region_5.0 | all-reduce | flops 512 | bytes 4096 | tf_op jit(solution)/shard_map/psum | solution.py:86
  74.9 59.5 %all-reduce = (f32[16,16]{1,0:T(8,128)S(1)}, f32[16,16]{1,0:T(8,128)S(1)}) all-reduce(f32[16,16]{1,0:T(8,128)S(1)} %get-tuple-element.19, f32[16,16]{1,0:T(8,128)S(1)} %get-tuple-element.20), channel_id=1, replica_groups=mesh['blk'=16,'sub'=2] {'blk'}, use_global_device_ids=true, to_apply=%region_6.7 | all-reduce | flops 512 | bytes 4096 | tf_op jit(solution)/shard_map/psum | solution.py:86
  134.4 1.5 cholesky.15
  135.9 0.6 compare_reduce_fusion
  136.5 0.6 fusion.22
  137.2 1.2 custom-call.8
  138.4 0.2 fusion.25
  138.6 0.2 fusion.23
  138.8 1.9 %convolution_subtract_fusion = f32[8,8192]{1,0:T(8,128)} fusion(bf16[16,8192]{1,0:T(8,128)(2,1)S(1)} %all_gather.3, f32[8,8192]{1,0:T(8,128)} %reduce-scatter.2.cloned.1.call-done, bf16[8,8192]{1,0:T(8,128)(2,1)S(1)} %copy-done.1, f32[8192]{0:T(1024)S(1)} %copy-done.2, f32[16,16]{0,1:T(8,128)S(1)} %fusion.23, s32[]{:T(128)S(6)} %select_n.42), kind=kOutput, calls=%fused_computation.2 | convolution fusion | flops 12845056 | bytes 954372 | tf_op jit(solution)/shard_map/dot_general | solution.py:90
  (34 shorter events, 1.1 us)
Async XLA Ops:
  6.5 15.1 %copy-start = (bf16[1,64,128,128]{3,2,1,0:T(8,128)(2,1)S(1)}, bf16[1,64,128,128]{3,2,1,0:T(8,128)(2,1)}, u32[]{:S(2)}) copy-start(bf16[1,64,128,128]{3,2,1,0:T(8,128)(2,1)} %param.11) | copy-start | bytes 6291460
  6.5 15.8 %copy-start.4 = (s32[1,64]{1,0:T(1,128)S(1)}, s32[1,64]{1,0:T(1,128)}, u32[]{:S(2)}) copy-start(s32[1,64]{1,0:T(1,128)} %param.13) | copy-start | bytes 772
  6.5 59.7 %reduce-scatter.2.cloned.1.call-start = ((), (), s32[]{:S(2)}) async-start(), calls=%async_computation.1 | async-start | bytes 786432 | tf_op jit(solution)/shard_map/reduce_scatter | solution.py:77
  14.1 15.0 %collective-permute-start.1 = (bf16[16,8192]{1,0:T(8,128)(2,1)S(1)}, bf16[16,8192]{1,0:T(8,128)(2,1)S(1)}, u32[]{:S(2)}, u32[]{:S(2)}) collective-permute-start(bf16[16,8192]{1,0:T(8,128)(2,1)S(1)} %all_gather.3), channel_id=1, source_target_pairs={{0,4},{2,6},{4,8},{6,10},{8,12},{10,14},{12,16},{14,18},{16,20},{1... | collective-permute-start | bytes 786440 | tf_op jit(solution)/shard_map/ppermute | solution.py:12
  17.6 11.6 %collective-permute-start = (bf16[16,8192]{1,0:T(8,128)(2,1)S(1)}, bf16[16,8192]{1,0:T(8,128)(2,1)S(1)}, u32[]{:S(2)}, u32[]{:S(2)}) collective-permute-start(bf16[16,8192]{1,0:T(8,128)(2,1)S(1)} %all_gather.3), channel_id=1, source_target_pairs={{0,2},{2,4},{4,6},{6,8},{8,10},{10,12},{12,14},{14,16},{16,18},{18... | collective-permute-start | bytes 786440 | tf_op jit(solution)/shard_map/ppermute | solution.py:12
  23.9 5.1 %copy-start.5 = (s32[1,64]{1,0:T(1,128)S(1)}, s32[1,64]{1,0:T(1,128)}, u32[]{:S(2)}) copy-start(s32[1,64]{1,0:T(1,128)} %param.14) | copy-start | bytes 772
  25.0 16.0 %collective-permute-start.3 = (f32[16,8192]{1,0:T(8,128)}, f32[16,8192]{1,0:T(8,128)}, u32[]{:S(2)}, u32[]{:S(2)}) collective-permute-start(f32[16,8192]{1,0:T(8,128)} %bitcast.93), channel_id=1, source_target_pairs={{4,0},{6,2},{8,4},{10,6},{12,8},{14,10},{16,12},{18,14},{20,16},{2... | collective-permute-start | bytes 1572872 | tf_op jit(solution)/shard_map/ppermute | solution.py:12
  27.5 13.6 %collective-permute-start.2 = (f32[16,8192]{1,0:T(8,128)}, f32[16,8192]{1,0:T(8,128)}, u32[]{:S(2)}, u32[]{:S(2)}) collective-permute-start(f32[16,8192]{1,0:T(8,128)} %bitcast.94), channel_id=1, source_target_pairs={{2,0},{4,2},{6,4},{8,6},{10,8},{12,10},{14,12},{16,14},{18,16},{20... | collective-permute-start | bytes 1572872 | tf_op jit(solution)/shard_map/ppermute | solution.py:12
  30.5 3.1 %copy-start.3 = (s32[1,64]{1,0:T(1,128)S(1)}, s32[1,64]{1,0:T(1,128)}, u32[]{:S(2)}) copy-start(s32[1,64]{1,0:T(1,128)} %param.12) | copy-start | bytes 772
  33.6 10.1 %copy-start.1 = (bf16[8,8192]{1,0:T(8,128)(2,1)S(1)}, bf16[8,8192]{1,0:T(8,128)(2,1)}, u32[]{:S(2)}) copy-start(bf16[8,8192]{1,0:T(8,128)(2,1)} %param.9) | copy-start | bytes 393220
  33.6 32.7 %copy-start.2 = (f32[8192]{0:T(1024)S(1)}, f32[8192]{0:T(1024)}, u32[]{:S(2)}) copy-start(f32[8192]{0:T(1024)} %param.10) | copy-start | bytes 98308
Sparse Core Ops, SparseCore 0:
  43.8 22.4 reduce-scatter.1
